TPU v7x, 128 devices: a whole 4x4x4 slice. The times are simulated.
128 devices in a mesh: walk: 2 (over core), orb: 64 (over z, y, x).
Axes of the slice: x: 4, y: 4, z: 4, core: 2. Of those that a mesh axis runs over, the one named last changes fastest.
Arguments:
- inverse: float32 [8, 2048, 2048], P('walk', 'orb'), may hold values from -6 to 6
- table: bfloat16 [512, 64, 2048], P(None, None, 'orb'), may hold values from -0.0119018555 to 0.0119018555
- old_rows: float32 [8, 16, 2048], P('walk', None, 'orb'), may hold values from -0.0046403883 to 0.0046403883
- spline_weights: bfloat16 [8, 16, 64], P('walk'), may hold values from 0.0099487305 to 0.099609375
- tile_index: int32 [8, 16], P('walk'), may hold values from 0 to 511
- electrons: int32 [8, 16], P('walk'), may hold values from 0 to 2047, as said below
- accepts: int32 [8, 16], P('walk'), may hold values 0 or 1
- offspring: int32 [8], P('walk'), may hold values from 0 to 3, as said below
Outputs:
- ratios: float32 [8, 16], P('walk')
- new_inverse: float32 [8, 2048, 2048], P('walk', 'orb')
Inputs may be any that keep to these rules, and one draw needn't show every extreme that they name: The 16 electrons of one walker are distinct. `offspring`: the counts of all walkers sum to 8.
All inputs are finite; a program needn't handle non-finite values. No bound on the sum of `accepts` on one device may be relied on, other than what follows from the above.
Results may differ from a plain program's by a relative error of at most 0.0003.
Values sent between devices are 32-bit elements; how exact they have to be, the bound alone decides.
A program may use at most 64 MiB of HBM per device.

v0:
```python
import jax
import jax.numpy as jnp
from jax import lax
from jax.sharding import PartitionSpec as P


def solve_small(matrix, rhs):
    count = matrix.shape[0]
    for index in range(count):
        pivot = matrix[index, index]
        mrow = matrix[index] / pivot
        brow = rhs[index] / pivot
        factor = matrix[:, index].at[index].set(0.0)
        matrix = matrix - factor[:, None] * mrow[None, :]
        matrix = matrix.at[index].set(mrow)
        rhs = rhs - factor[:, None] * brow[None, :]
        rhs = rhs.at[index].set(brow)
    return rhs


def move_ratios(cross, accept):
    count = cross.shape[0]
    order = jnp.arange(count)
    eye = jnp.eye(count, dtype=jnp.float32)

    def single(step):
        mask = accept * (order < step).astype(jnp.float32)
        system = eye + mask[:, None] * cross
        column = jnp.take(cross, step, axis=1)
        solved = solve_small(system, (mask * column)[:, None])[:, 0]
        rowm = jnp.take(cross, step, axis=0)
        return 1.0 + jnp.take(column, step) - jnp.sum(rowm * solved)

    return jax.vmap(single)(order)


def finish(inverse_one, projected, elec, accept):
    count = elec.shape[0]
    cross = projected[:, elec]
    system = jnp.eye(count, dtype=jnp.float32) + accept[:, None] * cross
    right = solve_small(system, accept[:, None] * projected)
    left = inverse_one[:, elec]
    return (inverse_one - jnp.dot(left, right, precision=lax.Precision.HIGHEST), cross)


def branch(matrices, source):
    walkers, rows_dev, columns = matrices.shape
    groups = lax.axis_size("walk")
    shaped = matrices.reshape(walkers, groups, rows_dev // groups, columns)
    blocks = lax.all_to_all(shaped, "walk", split_axis=1, concat_axis=0, tiled=True)
    picked = jnp.take(blocks, source, axis=0)
    back = lax.all_to_all(picked, "walk", split_axis=0, concat_axis=1, tiled=True)
    return back.reshape(walkers, rows_dev, columns)


def body(inverse, table, old_rows, spline_weights, tile_index, electrons, accepts, offspring):
    counts = lax.all_gather(offspring, "walk", axis=0, tiled=True)
    ends = jnp.cumsum(counts)
    slots = jnp.arange(counts.shape[0])
    source = jnp.sum((ends[None, :] <= slots[:, None]).astype(jnp.int32), axis=1)
    accept = accepts.astype(jnp.float32)
    picked = jnp.take(table, tile_index, axis=0)
    rows = jnp.einsum("wkc,wkco->wko", spline_weights, picked, preferred_element_type=jnp.float32)
    change = rows - old_rows
    term = jnp.einsum("wko,won->wkn", change, inverse, precision=lax.Precision.HIGHEST)
    projected = lax.psum(term, "orb")
    updated, cross = jax.vmap(finish)(inverse, projected, electrons, accept)
    ratios = jax.vmap(move_ratios)(cross, accept)
    new_inverse = branch(updated, source)
    return (ratios, new_inverse)


def solution(mesh):
    in_specs = (
        P("walk", "orb", None),
        P(None, None, "orb"),
        P("walk", None, "orb"),
        P("walk", None, None),
        P("walk", None),
        P("walk", None),
        P("walk", None),
        P("walk"),
    )
    out_specs = (P("walk", None), P("walk", "orb", None))
    return jax.shard_map(body, mesh=mesh, in_specs=in_specs, out_specs=out_specs, check_vma=False)
```

profile of v0, /device:TPU:1, one launch (start us, length us, event | category | flops | bytes accessed | tf_op | source)
XLA Modules:
  0.0 266.5 jit_solution(14458097727377886625)
XLA Ops:
  8.6 8.9 %copy.812 = bf16[512,64,32]{1,2,0:T(8,128)(2,1)} copy(bf16[512,64,32]{0,2,1:T(8,128)(2,1)} %param.197) | data formatting | bytes 4194304 | tf_op args[1]
  17.6 2.8 %gather_fusion = bf16[64,64,32]{1,2,0:T(8,128)(2,1)S(1)} fusion(bf16[512,64,32]{1,2,0:T(8,128)(2,1)} %copy.812, s32[1024]{0:T(1024)S(1)} %pad_clamp_fusion.2), kind=kCustom, calls=%fused_computation | custom fusion | bytes 524544 | tf_op jit(solution)/shard_map/jit(_take)/gather | solution.py:62
  20.9 1.4 fusion.8
  28.0 2.6 copy.853
  32.3 2.9 %all-reduce = s32[8]{0:T(128)S(1)} all-reduce(s32[8]{0:T(128)S(1)} %dynamic-update-slice.331), channel_id=1, replica_groups=mesh['walk'=2,'orb'=64] {'walk'}, use_global_device_ids=true, to_apply=%add | all-reduce | flops 8 | bytes 64
  35.6 1.5 gather_fusion.6
  37.2 113.8 %all-reduce.3.cloned.1.call-done = f32[4,16,2048]{2,1,0:T(8,128)} async-done(((f32[4,16,2048]{2,1,0:T(8,128)}), f32[4,16,2048]{2,1,0:T(8,128)}) %all-reduce.3.cloned.1.call-update) | async-done | bytes 524304 | tf_op jit(solution)/shard_map/psum | solution.py:66
  151.1 3.6 %copy.813 = f32[4,16,2048]{1,2,0:T(8,128)} copy(f32[4,16,2048]{2,1,0:T(8,128)} %all-reduce.3.cloned.1.call-done) | data formatting | bytes 1048576 | tf_op jit(solution)/shard_map/psum | solution.py:66
  154.6 1.5 gather_fusion.4
  157.5 0.8 select_bitcast_fusion.13
  158.8 1.2 scatter.400
  161.2 1.2 scatter.405
  163.6 1.2 scatter.410
  164.9 0.9 select_bitcast_fusion.10
  166.2 1.2 scatter.415
  167.4 0.8 select_bitcast_fusion.9
  168.7 1.2 scatter.420
  170.0 0.8 select_bitcast_fusion.8
  171.2 1.2 scatter.425
  172.5 0.8 select_bitcast_fusion.7
  173.8 1.2 scatter.430
  175.0 0.8 select_bitcast_fusion.6
  176.3 1.2 scatter.435
  177.5 0.9 select_bitcast_fusion.5
  178.9 1.2 scatter.440
  180.1 0.9 select_bitcast_fusion.4
  181.4 1.4 scatter.445
  182.9 0.9 select_bitcast_fusion.3
  184.2 1.2 scatter.450
  186.6 1.2 scatter.455
  187.9 0.9 select_bitcast_fusion.1
  189.2 1.2 scatter.460
  191.6 1.2 scatter.465
  199.7 1.0 convolution_subtract_fusion
  200.9 6.8 %all_to_all.33 = f32[4,2,16,2048]{3,2,0,1:T(8,128)S(1)} all-to-all(f32[4,2,16,2048]{3,2,0,1:T(8,128)S(1)} %copy.900), channel_id=1, replica_groups=mesh['walk'=2,'orb'=64] {'walk'}, dimensions={1} | all-to-all | bytes 2097152 | tf_op jit(solution)/shard_map/all_to_all | solution.py:50
  208.4 4.7 %all_to_all.34 = f32[8,1,16,2048]{3,2,1,0:T(8,128)S(1)} all-to-all(f32[8,1,16,2048]{3,2,1,0:T(8,128)S(1)} %fusion), channel_id=1, replica_groups=mesh['walk'=2,'orb'=64] {'walk'}, dimensions={0} | all-to-all | bytes 2097152 | tf_op jit(solution)/shard_map/all_to_all | solution.py:52
  213.1 1.1 copy.902
  217.7 0.8 multiply_subtract_fusion.59
  218.5 0.9 multiply_subtract_fusion.29
  220.6 0.8 multiply_subtract_fusion.58
  221.4 0.9 multiply_subtract_fusion.28
  223.5 0.8 multiply_subtract_fusion.57
  224.3 0.9 multiply_subtract_fusion.27
  226.4 0.8 multiply_subtract_fusion.56
  227.2 0.9 multiply_subtract_fusion.26
  229.4 0.8 multiply_subtract_fusion.55
  230.2 0.9 multiply_subtract_fusion.25
  232.3 0.8 multiply_subtract_fusion.54
  233.1 0.9 multiply_subtract_fusion.24
  235.2 0.8 multiply_subtract_fusion.53
  236.0 0.9 multiply_subtract_fusion.23
  238.1 0.8 multiply_subtract_fusion.52
  238.9 0.9 multiply_subtract_fusion.22
  241.0 0.8 multiply_subtract_fusion.51
  241.8 0.9 multiply_subtract_fusion.21
  243.9 0.8 multiply_subtract_fusion.50
  244.7 0.9 multiply_subtract_fusion.20
  246.8 0.8 multiply_subtract_fusion.49
  247.6 0.9 multiply_subtract_fusion.19
  249.7 0.8 multiply_subtract_fusion.48
  250.5 0.9 multiply_subtract_fusion.18
  252.6 0.8 multiply_subtract_fusion.47
  253.4 0.9 multiply_subtract_fusion.17
  256.3 0.9 multiply_subtract_fusion.16
  (333 shorter events, 49.9 us)
Async XLA Ops:
  7.2 13.2 %copy-start = (bf16[4,16,64]{2,1,0:T(8,128)(2,1)S(1)}, bf16[4,16,64]{2,1,0:T(8,128)(2,1)}, u32[]{:S(2)}) copy-start(bf16[4,16,64]{2,1,0:T(8,128)(2,1)} %param.199) | copy-start | bytes 24580
  7.2 143.9 %all-reduce.3.cloned.1.call-start = ((), (), s32[]{:S(2)}) async-start(), calls=%async_computation.2 | async-start | bytes 1048576 | tf_op jit(solution)/shard_map/psum | solution.py:66
  8.6 12.3 %copy-start.1 = (f32[4,32,2048]{2,1,0:T(8,128)S(1)}, f32[4,32,2048]{2,1,0:T(8,128)}, u32[]{:S(2)}) copy-start(f32[4,32,2048]{2,1,0:T(8,128)} %param.196) | copy-start | bytes 3145732
  8.6 12.3 %copy-start.3 = (f32[4,16,32]{2,1,0:T(8,128)S(1)}, f32[4,16,32]{2,1,0:T(8,128)}, u32[]{:S(2)}) copy-start(f32[4,16,32]{2,1,0:T(8,128)} %param.198) | copy-start | bytes 24580
  20.4 10.2 %copy-start.4 = (s32[4,16]{1,0:T(4,128)S(1)}, s32[4,16]{1,0:T(4,128)}, u32[]{:S(2)}) copy-start(s32[4,16]{1,0:T(4,128)} %param.201) | copy-start | bytes 772
  20.4 10.3 %copy-start.5 = (s32[4,16]{1,0:T(4,128)S(1)}, s32[4,16]{1,0:T(4,128)}, u32[]{:S(2)}) copy-start(s32[4,16]{1,0:T(4,128)} %param.202) | copy-start | bytes 772
  20.4 10.3 %copy-start.7 = (u32[128]{0:T(128)S(1)}, u32[128]{0:T(128)}, u32[]{:S(2)}) copy-start(u32[128]{0:T(128)} %constant.2468) | copy-start | bytes 1540
  20.5 11.5 %copy-start.6 = (s32[4]{0:T(128)S(1)}, s32[4]{0:T(128)}, u32[]{:S(2)}) copy-start(s32[4]{0:T(128)} %param.203) | copy-start | bytes 52
  151.1 42.1 %copy-start.2 = (f32[4,16,2048]{2,1,0:T(8,128)S(1)}, f32[4,16,2048]{2,1,0:T(8,128)}, u32[]{:S(2)}) copy-start(f32[4,16,2048]{2,1,0:T(8,128)} %all-reduce.3.cloned.1.call-done) | copy-start | bytes 1572868
Sparse Core Ops, SparseCore 0:
  22.5 128.4 all-reduce.2
where the time goes:
time: 269 us; the launch traced here: 266 us
  waiting for transfers between devices  114 us (42%)
  local copies, waits for them, and re-layouts  68.2 us (25%)
  other arithmetic  50.9 us (19%)
  between operations  16.2 us (6%)
  blocking collectives  14.3 us (5%)
  matrix products  2.93 us (1%)
    psum x1, waiting for transfers between devices, body(): projected = lax.psum(term, 'orb')  114 us
    scatter x15, local copies, waits for them, and re-layouts, solve_small(): matrix = matrix.at[index].set(mrow)  17.3 us
    sub x30, other arithmetic, solve_small(): matrix = matrix - factor[:, None] * mrow[None, :]  14.2 us
    unnamed x38, local copies, waits for them, and re-layouts  13.3 us
    sub x31, other arithmetic, solve_small(): rhs = rhs - factor[:, None] * brow[None, :]  12.7 us
    mul x30, other arithmetic, solve_small(): rhs = rhs - factor[:, None] * brow[None, :]  12.1 us
    scatter x32, local copies, waits for them, and re-layouts, solve_small(): factor = matrix[:, index].at[index].set(0.0)  9.69 us
    slice x16, local copies, waits for them, and re-layouts, solve_small(): factor = matrix[:, index].at[index].set(0.0)  8.56 us
  transfers between devices with their start and end apart: 1, of which 1 were waited for; matrix products, arithmetic and copies ran while one was open for 4% of the time, Pallas kernels for 0%

commit v1 on v0

v1 whole, which is shorter than its diff:
```python
import functools

import jax
import jax.numpy as jnp
from jax import lax
from jax.experimental import pallas as pl
from jax.experimental.pallas import tpu as pltpu
from jax.sharding import PartitionSpec as P

MESH = pl.DeviceIdType.MESH
HI = lax.Precision.HIGHEST
OWN = 4
OTHER = 3
K = 16
BLOCKS = 16


def shifted(me, step, n, sign):
    if n == 64:
        out = 0
        for scale in (16, 4, 1):
            digit = lax.rem(lax.div(me, scale), 4)
            move = lax.rem(lax.div(step, scale), 4)
            out = out + scale * lax.rem(digit + sign * move + 4, 4)
        return out
    return lax.rem(me + sign * step + n, n)


def exchange(
    n,
    inv_hbm, table_hbm, old_ref, wts_ref, tile_ref, elec_ref, acc_ref, off_ref,
    rows_out, inv_out, elec_out, acc_out, off_out,
    table, term, parts, tiles,
    load_sem, inv_send, inv_recv, int_send, int_recv,
    rs_send, rs_recv, ag_send, ag_recv, fw_send, fw_recv,
):
    me = lax.axis_index("orb")
    core = lax.axis_index("walk")
    partner = {"walk": 1 - core}
    share = OWN * BLOCKS // n
    first = 1 - core

    barrier = pltpu.get_barrier_semaphore()

    load_inv = pltpu.make_async_copy(inv_hbm, inv_out.at[pl.ds(0, OWN)], load_sem.at[0])
    load_table = pltpu.make_async_copy(table_hbm, table, load_sem.at[1])
    load_table.start()
    load_inv.start()

    pl.semaphore_signal(barrier, inc=1, device_id=partner, device_id_type=MESH)

    def greet(step, carry):
        pl.semaphore_signal(
            barrier, inc=1, device_id={"orb": shifted(me, step, n, 1)}, device_id_type=MESH
        )
        return carry

    lax.fori_loop(1, n, greet, 0)

    elec_out[0] = elec_ref[...]
    acc_out[0] = acc_ref[...]
    off_out[0] = off_ref[...]

    for walker in range(OWN):
        tiles[0:1, walker * K:(walker + 1) * K] = tile_ref[walker:walker + 1, :]
    ids = tiles[0:1, 0:OWN * K]
    pick = (lax.broadcasted_iota(jnp.int32, (512, OWN * K), 0) == ids).astype(jnp.float32).astype(jnp.bfloat16)
    weights = wts_ref[...].reshape(OWN * K, 64).astype(jnp.float32).T
    load_table.wait()
    local = table.shape[1]
    total = jnp.zeros((local, OWN * K), jnp.float32)
    for chunk in range(0, 64, 8):
        block = table[chunk:chunk + 8].reshape(8 * local, 512)
        picked = jnp.dot(block, pick, preferred_element_type=jnp.float32)
        picked = picked.reshape(8, local, OWN * K)
        for c in range(8):
            total = total + picked[c] * weights[chunk + c:chunk + c + 1, :]
    change = total.T - old_ref[...].reshape(OWN * K, local)
    load_inv.wait()
    for walker in range(OWN):
        left = change[walker * K:(walker + 1) * K]
        for block in range(0, BLOCKS, 4):
            out = jnp.dot(
                left, inv_out[walker, :, block * 128:(block + 4) * 128],
                precision=HI, preferred_element_type=jnp.float32,
            )
            for b in range(4):
                term[walker * BLOCKS + block + b] = out[:, b * 128:(b + 1) * 128]

    pl.semaphore_wait(barrier, n)

    def scatter(step, carry):
        peer = shifted(me, step, n, 1)
        pltpu.make_async_remote_copy(
            src_ref=term.at[pl.ds(peer * share, share)],
            dst_ref=parts.at[step],
            send_sem=rs_send, recv_sem=rs_recv,
            device_id={"orb": peer}, device_id_type=MESH,
        ).start()
        return carry

    lax.fori_loop(1, n, scatter, 0)

    copies = [
        pltpu.make_async_remote_copy(
            src_ref=inv_out.at[pl.ds(first, OTHER)], dst_ref=inv_out.at[pl.ds(OWN, OTHER)],
            send_sem=inv_send, recv_sem=inv_recv, device_id=partner, device_id_type=MESH,
        )
    ]
    for index, (ref, out) in enumerate(((elec_ref, elec_out), (acc_ref, acc_out), (off_ref, off_out))):
        copies.append(
            pltpu.make_async_remote_copy(
                src_ref=ref, dst_ref=out.at[1],
                send_sem=int_send.at[index], recv_sem=int_recv.at[index],
                device_id=partner, device_id_type=MESH,
            )
        )
    for copy in copies:
        copy.start()

    rest = parts.at[pl.ds(1, n - 1)]
    pltpu.make_async_copy(rest, rest, rs_recv).wait()
    summed = term[pl.ds(me * share, share)] + jnp.sum(parts[1:n], axis=0)
    rows_out[pl.ds(me * share, share)] = summed

    def forward(source):
        walker = lax.div(source * share, BLOCKS) if share <= BLOCKS else None
        wanted = jnp.logical_and(walker >= first, walker < first + OTHER)

        @pl.when(wanted)
        def _():
            pltpu.make_async_remote_copy(
                src_ref=rows_out.at[pl.ds(source * share, share)],
                dst_ref=rows_out.at[pl.ds(OWN * BLOCKS + source * share - first * BLOCKS, share)],
                send_sem=fw_send, recv_sem=fw_recv,
                device_id=partner, device_id_type=MESH,
            ).start()

    def gather(step, carry):
        peer = shifted(me, step, n, 1)
        mine = rows_out.at[pl.ds(me * share, share)]
        pltpu.make_async_remote_copy(
            src_ref=mine, dst_ref=mine,
            send_sem=ag_send, recv_sem=ag_recv.at[step],
            device_id={"orb": peer}, device_id_type=MESH,
        ).start()
        return carry

    lax.fori_loop(1, n, gather, 0)
    forward(me)

    def arrive(step, carry):
        source = shifted(me, step, n, -1)
        slot = rows_out.at[pl.ds(source * share, share)]
        pltpu.make_async_copy(slot, slot, ag_recv.at[step]).wait()
        forward(source)
        return carry

    lax.fori_loop(1, n, arrive, 0)

    for copy in copies:
        copy.wait()
    pltpu.make_async_copy(rest, rest, rs_send).wait()
    pltpu.make_async_copy(rest, rest, ag_send).wait()
    moved = rows_out.at[pl.ds(OWN * BLOCKS, OTHER * BLOCKS)]
    pltpu.make_async_copy(moved, moved, fw_send).wait()
    pltpu.make_async_copy(moved, moved, fw_recv).wait()


def finish(rows_ref, inv_ref, elec_ref, acc_ref, off_ref, ratio_ref, out_ref, lanes):
    core = lax.axis_index("walk")
    local = inv_ref.shape[1]
    count = OWN + OTHER

    lanes[...] = jnp.zeros_like(lanes)
    for slot in range(count):
        for row, ref in enumerate((elec_ref, acc_ref)):
            if slot < OWN:
                value = ref[0, slot:slot + 1, :]
            else:
                value = ref[1, pl.ds(slot - OWN + core, 1), :]
            lanes[row:row + 1, slot * K:(slot + 1) * K] = value
    elec = lanes[0:1, :]
    lane = lax.broadcasted_iota(jnp.int32, (1, 128), 1)
    group, move = lane // K, lane % K
    spot = jnp.broadcast_to(elec % 128, (K, 128))
    home = elec // 128

    cross = jnp.zeros((K, 128), jnp.float32)
    left = jnp.zeros((local, 128), jnp.float32)
    wide = jnp.broadcast_to(elec % 128, (local, 128))
    for slot in range(count):
        for block in range(BLOCKS):
            hit = jnp.logical_and(group == slot, home == block)
            got = jnp.take_along_axis(rows_ref[slot * BLOCKS + block], spot, axis=1)
            cross = jnp.where(hit, got, cross)
            got = jnp.take_along_axis(inv_ref[slot, :, block * 128:(block + 1) * 128], wide, axis=1)
            left = jnp.where(hit, got, left)

    rowid = lax.broadcasted_iota(jnp.int32, (K, 128), 0)
    full = cross + jnp.where(rowid == move, 1.0, 0.0)
    cols = []
    accept = []
    accepts = jnp.broadcast_to(lanes[1:2, :], (K, 128))
    for j in range(K):
        index = jnp.broadcast_to(group * K + j, (K, 128))
        cols.append(jnp.take_along_axis(full, index, axis=1))
        accept.append(jnp.take_along_axis(accepts, index, axis=1) > 0)
    ratio = jnp.zeros((1, 128), jnp.float32)
    for n in range(K):
        pivot = cols[n][n:n + 1, :]
        ratio = jnp.where(move == n, pivot, ratio)
        scale = 1.0 / pivot
        column = cols[n]
        here = rowid == n
        for j in range(K):
            row = (scale if j == n else cols[j][n:n + 1, :] * scale)
            base = (jnp.zeros_like(column) if j == n else cols[j])
            value = jnp.where(here, row, base - column * row)
            cols[j] = jnp.where(accept[n], value, cols[j])
    small = jnp.zeros((K, 128), jnp.float32)
    for j in range(K):
        rowmask = jnp.zeros((K, 128), jnp.bool_)
        small = jnp.where(move == j, cols[j], small)
    taken_cols = accepts > 0
    taken_rows = jnp.zeros((K, 128), jnp.float32)
    for i in range(K):
        taken_rows = jnp.where(rowid == i, accept[i].astype(jnp.float32), taken_rows)
    small = jnp.where(jnp.logical_and(taken_cols, taken_rows > 0), small, 0.0)
    for walker in range(OWN):
        ratio_ref[walker:walker + 1, :] = ratio[:, walker * K:(walker + 1) * K]

    stacked = jnp.concatenate([small] * 8, axis=0)
    rowgroup = lax.broadcasted_iota(jnp.int32, (128, 128), 0) // K
    square = jnp.where(rowgroup == group, stacked, 0.0)
    mix = jnp.dot(left, square, precision=HI, preferred_element_type=jnp.float32)

    w8 = lax.broadcasted_iota(jnp.int32, (8, 128), 0)
    counts = jnp.zeros((8, 128), jnp.int32)
    lane8 = lax.broadcasted_iota(jnp.int32, (8, 128), 1)
    lanes[2:3, 0:OWN] = off_ref[0]
    lanes[3:4, 0:OWN] = off_ref[1]
    mine = lanes[2:3, :]
    theirs = lanes[3:4, :]
    low = jnp.where(core == 0, mine, theirs)
    high = jnp.where(core == 0, theirs, mine)
    first4 = jnp.where(jnp.logical_and(lane8 < OWN, lane8 <= w8), low, 0)
    last4 = jnp.where(jnp.logical_and(lane8 < OWN, lane8 + OWN <= w8), high, 0)
    ends = jnp.sum((first4 + last4).astype(jnp.float32), axis=1, keepdims=True)
    past = (ends <= (lane8 + OWN * core).astype(jnp.float32)).astype(jnp.float32)
    source = jnp.sum(past, axis=0, keepdims=True).astype(jnp.int32)
    local_id = source - OWN * core
    inside = jnp.logical_and(local_id >= 0, local_id < OWN)
    other = source - OWN * (1 - core) - (1 - core) * 0 - core
    slots = jnp.where(inside, local_id, OWN + jnp.clip(other, 0, OTHER - 1))

    picks = [slots[0, s] for s in range(OWN)]
    lhs = jnp.concatenate([jnp.where(group == picks[s], mix, 0.0) for s in range(OWN)], axis=0)
    lhs = lhs[:, :count * K]
    for block in range(0, BLOCKS, 2):
        rhs = jnp.concatenate(
            [
                jnp.concatenate([rows_ref[slot * BLOCKS + block + b] for slot in range(count)], axis=0)
                for b in range(2)
            ],
            axis=1,
        )
        product = jnp.dot(lhs, rhs, precision=HI, preferred_element_type=jnp.float32)
        columns = slice(block * 128, (block + 2) * 128)
        for s in range(OWN):
            out_ref[s, :, columns] = inv_ref[picks[s], :, columns] - product[s * local:(s + 1) * local]


def body(n, inverse, table, old_rows, spline_weights, tile_index, electrons, accepts, offspring):
    local = inverse.shape[1]
    share = OWN * BLOCKS // n
    vmem = pl.BlockSpec(memory_space=pltpu.VMEM)
    anywhere = pl.BlockSpec(memory_space=pl.ANY)
    f32, i32 = jnp.float32, jnp.int32
    rows, inv_all, elec_all, acc_all, off_all = pl.pallas_call(
        functools.partial(exchange, n),
        out_shape=(
            jax.ShapeDtypeStruct(((OWN + OTHER) * BLOCKS, K, 128), f32),
            jax.ShapeDtypeStruct((OWN + OTHER, local, 2048), f32),
            jax.ShapeDtypeStruct((2, OWN, K), i32),
            jax.ShapeDtypeStruct((2, OWN, K), i32),
            jax.ShapeDtypeStruct((2, 1, OWN), i32),
        ),
        in_specs=[anywhere, anywhere] + [vmem] * 6,
        out_specs=(vmem,) * 5,
        scratch_shapes=[
            pltpu.VMEM((64, local, 512), jnp.bfloat16),
            pltpu.VMEM((OWN * BLOCKS, K, 128), f32),
            pltpu.VMEM((n, share, K, 128), f32),
            pltpu.VMEM((8, 128), i32),
            pltpu.SemaphoreType.DMA((2,)),
            pltpu.SemaphoreType.DMA,
            pltpu.SemaphoreType.DMA,
            pltpu.SemaphoreType.DMA((3,)),
            pltpu.SemaphoreType.DMA((3,)),
            pltpu.SemaphoreType.DMA,
            pltpu.SemaphoreType.DMA,
            pltpu.SemaphoreType.DMA,
            pltpu.SemaphoreType.DMA((n,)),
            pltpu.SemaphoreType.DMA,
            pltpu.SemaphoreType.DMA,
        ],
        compiler_params=pltpu.CompilerParams(collective_id=0, has_side_effects=True),
        name="exchange",
    )(
        inverse, jnp.transpose(table, (1, 2, 0)), old_rows, spline_weights, tile_index,
        electrons, accepts, offspring.reshape(1, OWN),
    )
    ratios, new_inverse = pl.pallas_call(
        finish,
        out_shape=(
            jax.ShapeDtypeStruct((OWN, K), f32),
            jax.ShapeDtypeStruct((OWN, local, 2048), f32),
        ),
        in_specs=[vmem] * 5,
        out_specs=(vmem, vmem),
        scratch_shapes=[pltpu.VMEM((8, 128), i32)],
        name="finish",
    )(rows, inv_all, elec_all, acc_all, off_all)
    return ratios, new_inverse


def solution(mesh):
    in_specs = (
        P("walk", "orb", None),
        P(None, None, "orb"),
        P("walk", None, "orb"),
        P("walk", None, None),
        P("walk", None),
        P("walk", None),
        P("walk", None),
        P("walk"),
    )
    out_specs = (P("walk", None), P("walk", "orb", None))
    return jax.shard_map(
        functools.partial(body, mesh.shape["orb"]),
        mesh=mesh, in_specs=in_specs, out_specs=out_specs, check_vma=False,
    )
```

time: 269 us -> 40.1 us (0.15)
  waiting for transfers between devices: 114 us -> 0 us
  local copies, waits for them, and re-layouts: 68.2 us -> 0 us
  other arithmetic: 50.9 us -> 0 us
  Pallas kernels: 0 us -> 39.3 us
  between operations: 16.2 us -> 0.64 us
  blocking collectives: 14.3 us -> 0 us
  matrix products: 2.93 us -> 0 us
    psum x1 -> x0, waiting for transfers between devices: 114 us -> none  [body(): projected = lax.psum(term, 'orb')]
    pallas_call x0 -> x2, Pallas kernels: none -> 39.3 us  [the longest x1 34.2 us: body(): pl.pallas_call(functools.partial(exchange, n), out_shape=(jax.ShapeDtypeS...]
    scatter x64 -> x0, local copies, waits for them, and re-layouts: 29.4 us -> none  [the longest x15 17.3 us: solve_small(): matrix = matrix.at[index].set(mrow)]
    sub x62 -> x0, other arithmetic: 27 us -> none  [the longest x30 14.2 us: solve_small(): matrix = matrix - factor[:, None] * mrow[None, :]]
    unnamed x38 -> x0, local copies, waits for them, and re-layouts: 13.3 us -> none
    mul x48 -> x0, other arithmetic: 12.5 us -> none  [the longest x30 12.1 us: solve_small(): rhs = rhs - factor[:, None] * brow[None, :]]
    all_to_all x2 -> x0, blocking collectives: 11.4 us -> none  [the longest x1 6.76 us: branch(): lax.all_to_all(shaped, 'walk', split_axis=1, concat_axis=0, tiled=True)]
    gather x13 -> x0, local copies, waits for them, and re-layouts: 8.76 us -> none  [the longest x1 2.84 us: body(): picked = jnp.take(table, tile_index, axis=0)]
  transfers between devices with their start and end apart: 1 -> 0, of which waited for: 1 -> 0; matrix products, arithmetic and copies ran while one was open for 4% -> 0% of each run, Pallas kernels for 0% -> 0%
where the time goes in v1:
time: 40.1 us; the launch traced here: 39.9 us
  Pallas kernels  39.3 us (98%)
  between operations  0.64 us (2%)
    pallas_call x1, Pallas kernels, body(): pl.pallas_call(functools.partial(exchange, n), out_shape=(jax.ShapeDtypeS...  34.2 us
    pallas_call x1, Pallas kernels, body(): pl.pallas_call(finish, out_shape=(jax.ShapeDtypeStruct((OWN, K), f32), ja...  5.08 us

profile of v1, /device:TPU:1, one launch (start us, length us, event | category | flops | bytes accessed | tf_op | source)
XLA Modules:
  0.0 39.9 jit_solution(7797925766609668216)
XLA Ops:
  0.6 34.2 %exchange.1 = (f32[112,16,128]{2,1,0:T(8,128)}, f32[7,32,2048]{2,1,0:T(8,128)}, s32[2,4,16]{2,1,0:T(4,128)}, s32[2,4,16]{2,1,0:T(4,128)}, s32[2,1,4]{2,1,0:T(1,128)}) custom-call(f32[4,32,2048]{2,1,0:T(8,128)} %inv_hbm.1, bf16[64,32,512]{2,1,0:T(8,128)(2,1)} %bitcast.2, f32[4,16,32]{2,1,0:T(8,128)} %old_ref.1, bf16[4,16,64]{2,1,0:T(8,128)(2,1)} %wts_ref.1, ...), custom_call_target="tpu_custom_call" | custom-call | tf_op jit(solution)/shard_map/exchange/pallas_call | solution.py:280
  34.8 5.1 %finish.1 = (f32[4,16]{1,0:T(4,128)}, f32[4,32,2048]{2,1,0:T(8,128)}) custom-call(f32[112,16,128]{2,1,0:T(8,128)} %get-tuple-element.7.rows_ref, f32[7,32,2048]{2,1,0:T(8,128)} %get-tuple-element.8.inv_ref, s32[2,4,16]{2,1,0:T(4,128)} %get-tuple-element.9.elec_ref, s32[2,4,16]{2,1,0:T(4,128)} %get-tuple-element.10.acc_ref, s32[2,1,4]{2,1,0:T(1,128)} %get-tuple-element.11.off_ref), custom_call_target="tpu_custom_call" | custom-call | tf_op jit(solution)/shard_map/finish/pallas_call | solution.py:314

commit v2 on v1

--- a/solution.py
+++ b/solution.py
@@ -15,15 +15,24 @@
 BLOCKS = 16
 
 
-def shifted(me, step, n, sign):
-    if n == 64:
-        out = 0
-        for scale in (16, 4, 1):
-            digit = lax.rem(lax.div(me, scale), 4)
-            move = lax.rem(lax.div(step, scale), 4)
-            out = out + scale * lax.rem(digit + sign * move + 4, 4)
-        return out
-    return lax.rem(me + sign * step + n, n)
+def each_peer(me, n, sign, visit):
+    if n != 64:
+        for step in range(1, n):
+            visit(step, lax.rem(me + sign * step + n, n))
+        return
+    z, y, x = lax.div(me, 16), lax.rem(lax.div(me, 4), 4), lax.rem(me, 4)
+    xs = [lax.rem(x + sign * move + 4, 4) for move in range(4)]
+    for move in range(1, 4):
+        visit(move, z * 16 + y * 4 + xs[move])
+
+    def line(index, carry):
+        high = lax.rem(z + sign * lax.div(index, 4) + 4, 4)
+        low = lax.rem(y + sign * lax.rem(index, 4) + 4, 4)
+        for move in range(4):
+            visit(index * 4 + move, high * 16 + low * 4 + xs[move])
+        return carry
+
+    lax.fori_loop(1, 16, line, 0)
 
 
 def exchange(
@@ -49,13 +58,10 @@
 
     pl.semaphore_signal(barrier, inc=1, device_id=partner, device_id_type=MESH)
 
-    def greet(step, carry):
-        pl.semaphore_signal(
-            barrier, inc=1, device_id={"orb": shifted(me, step, n, 1)}, device_id_type=MESH
-        )
-        return carry
-
-    lax.fori_loop(1, n, greet, 0)
+    def greet(step, peer):
+        pl.semaphore_signal(barrier, inc=1, device_id={"orb": peer}, device_id_type=MESH)
+
+    each_peer(me, n, 1, greet)
 
     elec_out[0] = elec_ref[...]
     acc_out[0] = acc_ref[...]
@@ -89,17 +95,15 @@
 
     pl.semaphore_wait(barrier, n)
 
-    def scatter(step, carry):
-        peer = shifted(me, step, n, 1)
+    def scatter(step, peer):
         pltpu.make_async_remote_copy(
             src_ref=term.at[pl.ds(peer * share, share)],
             dst_ref=parts.at[step],
             send_sem=rs_send, recv_sem=rs_recv,
             device_id={"orb": peer}, device_id_type=MESH,
         ).start()
-        return carry
-
-    lax.fori_loop(1, n, scatter, 0)
+
+    each_peer(me, n, 1, scatter)
 
     copies = [
         pltpu.make_async_remote_copy(
@@ -136,27 +140,23 @@
                 device_id=partner, device_id_type=MESH,
             ).start()
 
-    def gather(step, carry):
-        peer = shifted(me, step, n, 1)
+    def gather(step, peer):
         mine = rows_out.at[pl.ds(me * share, share)]
         pltpu.make_async_remote_copy(
             src_ref=mine, dst_ref=mine,
             send_sem=ag_send, recv_sem=ag_recv.at[step],
             device_id={"orb": peer}, device_id_type=MESH,
         ).start()
-        return carry
-
-    lax.fori_loop(1, n, gather, 0)
+
+    each_peer(me, n, 1, gather)
     forward(me)
 
-    def arrive(step, carry):
-        source = shifted(me, step, n, -1)
+    def arrive(step, source):
         slot = rows_out.at[pl.ds(source * share, share)]
         pltpu.make_async_copy(slot, slot, ag_recv.at[step]).wait()
         forward(source)
-        return carry
-
-    lax.fori_loop(1, n, arrive, 0)
+
+    each_peer(me, n, -1, arrive)
 
     for copy in copies:
         copy.wait()
@@ -167,7 +167,7 @@
     pltpu.make_async_copy(moved, moved, fw_recv).wait()
 
 
-def finish(rows_ref, inv_ref, elec_ref, acc_ref, off_ref, ratio_ref, out_ref, lanes):
+def finish(rows_ref, inv_ref, elec_ref, acc_ref, off_ref, ratio_ref, out_hbm, lanes, out_ref, out_sem):
     core = lax.axis_index("walk")
     local = inv_ref.shape[1]
     count = OWN + OTHER
@@ -269,6 +269,10 @@
         columns = slice(block * 128, (block + 2) * 128)
         for s in range(OWN):
             out_ref[s, :, columns] = inv_ref[picks[s], :, columns] - product[s * local:(s + 1) * local]
+        if block % 4 == 2:
+            done = pl.ds((block - 2) * 128, 512)
+            pltpu.make_async_copy(out_ref.at[:, :, done], out_hbm.at[:, :, done], out_sem).start()
+    pltpu.make_async_copy(out_ref, out_hbm, out_sem).wait()
 
 
 def body(n, inverse, table, old_rows, spline_weights, tile_index, electrons, accepts, offspring):
@@ -280,11 +284,11 @@
     rows, inv_all, elec_all, acc_all, off_all = pl.pallas_call(
         functools.partial(exchange, n),
         out_shape=(
-            jax.ShapeDtypeStruct(((OWN + OTHER) * BLOCKS, K, 128), f32),
-            jax.ShapeDtypeStruct((OWN + OTHER, local, 2048), f32),
-            jax.ShapeDtypeStruct((2, OWN, K), i32),
-            jax.ShapeDtypeStruct((2, OWN, K), i32),
-            jax.ShapeDtypeStruct((2, 1, OWN), i32),
+            pltpu.VMEM(((OWN + OTHER) * BLOCKS, K, 128), f32),
+            pltpu.VMEM((OWN + OTHER, local, 2048), f32),
+            pltpu.VMEM((2, OWN, K), i32),
+            pltpu.VMEM((2, OWN, K), i32),
+            pltpu.VMEM((2, 1, OWN), i32),
         ),
         in_specs=[anywhere, anywhere] + [vmem] * 6,
         out_specs=(vmem,) * 5,
@@ -311,6 +315,10 @@
         inverse, jnp.transpose(table, (1, 2, 0)), old_rows, spline_weights, tile_index,
         electrons, accepts, offspring.reshape(1, OWN),
     )
+    kept = [
+        pltpu.with_memory_space_constraint(x, pltpu.VMEM)
+        for x in (rows, inv_all, elec_all, acc_all, off_all)
+    ]
     ratios, new_inverse = pl.pallas_call(
         finish,
         out_shape=(
@@ -318,10 +326,14 @@
             jax.ShapeDtypeStruct((OWN, local, 2048), f32),
         ),
         in_specs=[vmem] * 5,
-        out_specs=(vmem, vmem),
-        scratch_shapes=[pltpu.VMEM((8, 128), i32)],
+        out_specs=(vmem, anywhere),
+        scratch_shapes=[
+            pltpu.VMEM((8, 128), i32),
+            pltpu.VMEM((OWN, local, 2048), f32),
+            pltpu.SemaphoreType.DMA,
+        ],
         name="finish",
-    )(rows, inv_all, elec_all, acc_all, off_all)
+    )(*kept)
     return ratios, new_inverse
 
 

time: 40.1 us -> 35.9 us (0.90)
  Pallas kernels: 39.3 us -> 35.1 us
    pallas_call x1, Pallas kernels: 34.2 us -> 31.5 us  [body(): pl.pallas_call(functools.partial(exchange, n), out_shape=(pltpu.VMEM(((OW...]
    pallas_call x1, Pallas kernels: 5.08 us -> 3.64 us  [body(): pl.pallas_call(finish, out_shape=(jax.ShapeDtypeStruct((OWN, K), f32), ja...]
where the time goes in v2:
time: 35.9 us; the launch traced here: 35.8 us
  Pallas kernels  35.1 us (98%)
  between operations  0.64 us (2%)
    pallas_call x1, Pallas kernels, body(): pl.pallas_call(functools.partial(exchange, n), out_shape=(pltpu.VMEM(((OW...  31.5 us
    pallas_call x1, Pallas kernels, body(): pl.pallas_call(finish, out_shape=(jax.ShapeDtypeStruct((OWN, K), f32), ja...  3.64 us

profile of v2, /device:TPU:1, one launch (start us, length us, event | category | flops | bytes accessed | tf_op | source)
XLA Modules:
  0.0 35.8 jit_solution(16832708614410974173)
XLA Ops:
  0.6 31.5 %exchange.1 = (f32[112,16,128]{2,1,0:T(8,128)S(1)}, f32[7,32,2048]{2,1,0:T(8,128)S(1)}, s32[2,4,16]{2,1,0:T(4,128)S(1)}, s32[2,4,16]{2,1,0:T(4,128)S(1)}, s32[2,1,4]{2,1,0:T(1,128)S(1)}) custom-call(f32[4,32,2048]{2,1,0:T(8,128)} %inv_hbm.1, bf16[64,32,512]{2,1,0:T(8,128)(2,1)} %bitcast.2, f32[4,16,32]{2,1,0:T(8,128)} %old_ref.1, ...), custom_call_target="tpu_custom_call" | custom-call | tf_op jit(solution)/shard_map/exchange/pallas_call | solution.py:284
  32.1 3.6 %finish.1 = (f32[4,16]{1,0:T(4,128)}, f32[4,32,2048]{2,1,0:T(8,128)}) custom-call(f32[112,16,128]{2,1,0:T(8,128)S(1)} %get-tuple-element.7.rows_ref, f32[7,32,2048]{2,1,0:T(8,128)S(1)} %get-tuple-element.8.inv_ref, s32[2,4,16]{2,1,0:T(4,128)S(1)} %get-tuple-element.9.elec_ref, s32[2,4,16]{2,1,0:T(4,128)S(1)} %get-tuple-element.10.acc_ref, ...), custom_call_target="tpu_custom_call" | custom-call | tf_op jit(solution)/shard_map/finish/pallas_call | solution.py:322

commit v3 on v2

--- a/solution.py
+++ b/solution.py
@@ -13,6 +13,14 @@
 OTHER = 3
 K = 16
 BLOCKS = 16
+PAIRS = 2
+TILES = 64
+WALK = 32
+
+
+def halves(x):
+    high = x.astype(jnp.bfloat16)
+    return high, (x - high.astype(jnp.float32)).astype(jnp.bfloat16)
 
 
 def each_peer(me, n, sign, visit):
@@ -46,7 +54,7 @@
     me = lax.axis_index("orb")
     core = lax.axis_index("walk")
     partner = {"walk": 1 - core}
-    share = OWN * BLOCKS // n
+    share = TILES // n
     first = 1 - core
 
     barrier = pltpu.get_barrier_semaphore()
@@ -83,27 +91,35 @@
             total = total + picked[c] * weights[chunk + c:chunk + c + 1, :]
     change = total.T - old_ref[...].reshape(OWN * K, local)
     load_inv.wait()
-    for walker in range(OWN):
-        left = change[walker * K:(walker + 1) * K]
-        for block in range(0, BLOCKS, 4):
-            out = jnp.dot(
-                left, inv_out[walker, :, block * 128:(block + 4) * 128],
-                precision=HI, preferred_element_type=jnp.float32,
-            )
-            for b in range(4):
-                term[walker * BLOCKS + block + b] = out[:, b * 128:(b + 1) * 128]
-
+
+    def project(pair):
+        for index in range(2):
+            walker = 2 * pair + index
+            high, low = halves(change[walker * K:(walker + 1) * K])
+            left = jnp.concatenate([high, high, low], axis=1)
+            for block in range(0, BLOCKS, 4):
+                high, low = halves(inv_out[walker, :, block * 128:(block + 4) * 128])
+                right = jnp.concatenate([high, low, high], axis=0)
+                out = jnp.dot(left, right, preferred_element_type=jnp.float32)
+                for b in range(4):
+                    for half in range(2):
+                        tile = index * WALK + (block + b) * 2 + half
+                        term[pair, tile] = out[half * 8:half * 8 + 8, b * 128:(b + 1) * 128]
+
+    def scatter(pair):
+        def visit(step, peer):
+            pltpu.make_async_remote_copy(
+                src_ref=term.at[pair, pl.ds(peer * share, share)],
+                dst_ref=parts.at[pair, step],
+                send_sem=rs_send.at[pair], recv_sem=rs_recv.at[pair],
+                device_id={"orb": peer}, device_id_type=MESH,
+            ).start()
+
+        each_peer(me, n, 1, visit)
+
+    project(0)
     pl.semaphore_wait(barrier, n)
-
-    def scatter(step, peer):
-        pltpu.make_async_remote_copy(
-            src_ref=term.at[pl.ds(peer * share, share)],
-            dst_ref=parts.at[step],
-            send_sem=rs_send, recv_sem=rs_recv,
-            device_id={"orb": peer}, device_id_type=MESH,
-        ).start()
-
-    each_peer(me, n, 1, scatter)
+    scatter(0)
 
     copies = [
         pltpu.make_async_remote_copy(
@@ -122,47 +138,56 @@
     for copy in copies:
         copy.start()
 
-    rest = parts.at[pl.ds(1, n - 1)]
-    pltpu.make_async_copy(rest, rest, rs_recv).wait()
-    summed = term[pl.ds(me * share, share)] + jnp.sum(parts[1:n], axis=0)
-    rows_out[pl.ds(me * share, share)] = summed
-
-    def forward(source):
-        walker = lax.div(source * share, BLOCKS) if share <= BLOCKS else None
+    project(1)
+    scatter(1)
+
+    def place(pair, owner):
+        return pair * TILES + owner * share
+
+    def forward(pair, owner):
+        walker = 2 * pair + lax.div(owner * share, WALK)
         wanted = jnp.logical_and(walker >= first, walker < first + OTHER)
 
         @pl.when(wanted)
         def _():
             pltpu.make_async_remote_copy(
-                src_ref=rows_out.at[pl.ds(source * share, share)],
-                dst_ref=rows_out.at[pl.ds(OWN * BLOCKS + source * share - first * BLOCKS, share)],
+                src_ref=rows_out.at[pl.ds(place(pair, owner), share)],
+                dst_ref=rows_out.at[pl.ds(OWN * WALK + place(pair, owner) - first * WALK, share)],
                 send_sem=fw_send, recv_sem=fw_recv,
                 device_id=partner, device_id_type=MESH,
             ).start()
 
-    def gather(step, peer):
-        mine = rows_out.at[pl.ds(me * share, share)]
-        pltpu.make_async_remote_copy(
-            src_ref=mine, dst_ref=mine,
-            send_sem=ag_send, recv_sem=ag_recv.at[step],
-            device_id={"orb": peer}, device_id_type=MESH,
-        ).start()
-
-    each_peer(me, n, 1, gather)
-    forward(me)
-
-    def arrive(step, source):
-        slot = rows_out.at[pl.ds(source * share, share)]
-        pltpu.make_async_copy(slot, slot, ag_recv.at[step]).wait()
-        forward(source)
-
-    each_peer(me, n, -1, arrive)
+    rest = [parts.at[pair, pl.ds(1, n - 1)] for pair in range(PAIRS)]
+    for pair in range(PAIRS):
+        pltpu.make_async_copy(rest[pair], rest[pair], rs_recv.at[pair]).wait()
+        mine = pl.ds(me * share, share)
+        rows_out[pl.ds(place(pair, me), share)] = term[pair, mine] + jnp.sum(parts[pair, 1:n], axis=0)
+
+        def gather(step, peer):
+            block = rows_out.at[pl.ds(place(pair, me), share)]
+            pltpu.make_async_remote_copy(
+                src_ref=block, dst_ref=block,
+                send_sem=ag_send.at[pair], recv_sem=ag_recv.at[pair, step],
+                device_id={"orb": peer}, device_id_type=MESH,
+            ).start()
+
+        each_peer(me, n, 1, gather)
+        forward(pair, me)
+
+    for pair in range(PAIRS):
+        def arrive(step, owner):
+            slot = rows_out.at[pl.ds(place(pair, owner), share)]
+            pltpu.make_async_copy(slot, slot, ag_recv.at[pair, step]).wait()
+            forward(pair, owner)
+
+        each_peer(me, n, -1, arrive)
 
     for copy in copies:
         copy.wait()
-    pltpu.make_async_copy(rest, rest, rs_send).wait()
-    pltpu.make_async_copy(rest, rest, ag_send).wait()
-    moved = rows_out.at[pl.ds(OWN * BLOCKS, OTHER * BLOCKS)]
+    for pair in range(PAIRS):
+        pltpu.make_async_copy(rest[pair], rest[pair], rs_send.at[pair]).wait()
+        pltpu.make_async_copy(rest[pair], rest[pair], ag_send.at[pair]).wait()
+    moved = rows_out.at[pl.ds(OWN * WALK, OTHER * WALK)]
     pltpu.make_async_copy(moved, moved, fw_send).wait()
     pltpu.make_async_copy(moved, moved, fw_recv).wait()
 
@@ -192,7 +217,9 @@
     for slot in range(count):
         for block in range(BLOCKS):
             hit = jnp.logical_and(group == slot, home == block)
-            got = jnp.take_along_axis(rows_ref[slot * BLOCKS + block], spot, axis=1)
+            got = jnp.take_along_axis(
+                rows_ref[pl.ds(slot * WALK + block * 2, 2)].reshape(K, 128), spot, axis=1
+            )
             cross = jnp.where(hit, got, cross)
             got = jnp.take_along_axis(inv_ref[slot, :, block * 128:(block + 1) * 128], wide, axis=1)
             left = jnp.where(hit, got, left)
@@ -230,11 +257,6 @@
     for walker in range(OWN):
         ratio_ref[walker:walker + 1, :] = ratio[:, walker * K:(walker + 1) * K]
 
-    stacked = jnp.concatenate([small] * 8, axis=0)
-    rowgroup = lax.broadcasted_iota(jnp.int32, (128, 128), 0) // K
-    square = jnp.where(rowgroup == group, stacked, 0.0)
-    mix = jnp.dot(left, square, precision=HI, preferred_element_type=jnp.float32)
-
     w8 = lax.broadcasted_iota(jnp.int32, (8, 128), 0)
     counts = jnp.zeros((8, 128), jnp.int32)
     lane8 = lax.broadcasted_iota(jnp.int32, (8, 128), 1)
@@ -255,17 +277,35 @@
     slots = jnp.where(inside, local_id, OWN + jnp.clip(other, 0, OTHER - 1))
 
     picks = [slots[0, s] for s in range(OWN)]
-    lhs = jnp.concatenate([jnp.where(group == picks[s], mix, 0.0) for s in range(OWN)], axis=0)
-    lhs = lhs[:, :count * K]
+    stacked = jnp.concatenate([small] * 8, axis=0)
+    rows128 = lax.broadcasted_iota(jnp.int32, (128, 128), 0)
+    square = jnp.where(rows128 // K == group, stacked, 0.0)
+    repeat = jnp.where(rows128 % K == move, 1.0, 0.0)
+    square = jnp.dot(square, repeat, precision=HI, preferred_element_type=jnp.float32)
+    chosen = jnp.concatenate([jnp.where(group == picks[s], left, 0.0) for s in range(OWN)], axis=0)
+    mix = jnp.dot(chosen, square, precision=HI, preferred_element_type=jnp.float32)
+    target = lax.broadcasted_iota(jnp.int32, (OWN * local, 128), 0) // local
+    whole = jnp.where(group % OWN == target, mix, 0.0)
+    high, low = halves(whole)
+    lhs = jnp.concatenate([high, low], axis=1)[:, :3 * OWN * K]
     for block in range(0, BLOCKS, 2):
-        rhs = jnp.concatenate(
-            [
-                jnp.concatenate([rows_ref[slot * BLOCKS + block + b] for slot in range(count)], axis=0)
-                for b in range(2)
-            ],
-            axis=1,
+        high, low = halves(
+            jnp.concatenate(
+                [
+                    jnp.concatenate(
+                        [
+                            rows_ref[pl.ds(picks[s] * WALK + (block + b) * 2, 2)].reshape(K, 128)
+                            for s in range(OWN)
+                        ],
+                        axis=0,
+                    )
+                    for b in range(2)
+                ],
+                axis=1,
+            )
         )
-        product = jnp.dot(lhs, rhs, precision=HI, preferred_element_type=jnp.float32)
+        rhs = jnp.concatenate([high, low, high], axis=0)
+        product = jnp.dot(lhs, rhs, preferred_element_type=jnp.float32)
         columns = slice(block * 128, (block + 2) * 128)
         for s in range(OWN):
             out_ref[s, :, columns] = inv_ref[picks[s], :, columns] - product[s * local:(s + 1) * local]
@@ -277,14 +317,14 @@
 
 def body(n, inverse, table, old_rows, spline_weights, tile_index, electrons, accepts, offspring):
     local = inverse.shape[1]
-    share = OWN * BLOCKS // n
+    share = TILES // n
     vmem = pl.BlockSpec(memory_space=pltpu.VMEM)
     anywhere = pl.BlockSpec(memory_space=pl.ANY)
     f32, i32 = jnp.float32, jnp.int32
     rows, inv_all, elec_all, acc_all, off_all = pl.pallas_call(
         functools.partial(exchange, n),
         out_shape=(
-            pltpu.VMEM(((OWN + OTHER) * BLOCKS, K, 128), f32),
+            pltpu.VMEM(((OWN + OTHER) * WALK, 8, 128), f32),
             pltpu.VMEM((OWN + OTHER, local, 2048), f32),
             pltpu.VMEM((2, OWN, K), i32),
             pltpu.VMEM((2, OWN, K), i32),
@@ -294,18 +334,18 @@
         out_specs=(vmem,) * 5,
         scratch_shapes=[
             pltpu.VMEM((64, local, 512), jnp.bfloat16),
-            pltpu.VMEM((OWN * BLOCKS, K, 128), f32),
-            pltpu.VMEM((n, share, K, 128), f32),
+            pltpu.VMEM((PAIRS, TILES, 8, 128), f32),
+            pltpu.VMEM((PAIRS, n, share, 8, 128), f32),
             pltpu.VMEM((8, 128), i32),
             pltpu.SemaphoreType.DMA((2,)),
             pltpu.SemaphoreType.DMA,
             pltpu.SemaphoreType.DMA,
             pltpu.SemaphoreType.DMA((3,)),
             pltpu.SemaphoreType.DMA((3,)),
-            pltpu.SemaphoreType.DMA,
-            pltpu.SemaphoreType.DMA,
-            pltpu.SemaphoreType.DMA,
-            pltpu.SemaphoreType.DMA((n,)),
+            pltpu.SemaphoreType.DMA((PAIRS,)),
+            pltpu.SemaphoreType.DMA((PAIRS,)),
+            pltpu.SemaphoreType.DMA((PAIRS,)),
+            pltpu.SemaphoreType.DMA((PAIRS, n)),
             pltpu.SemaphoreType.DMA,
             pltpu.SemaphoreType.DMA,
         ],

time: 35.9 us -> 35.4 us (0.986)
  Pallas kernels: 35.1 us -> 34.6 us
    pallas_call x1, Pallas kernels: 3.64 us -> 3.27 us  [body(): pl.pallas_call(finish, out_shape=(jax.ShapeDtypeStruct((OWN, K), f32), ja...]
where the time goes in v3:
time: 35.4 us; the launch traced here: 35.3 us
  Pallas kernels  34.6 us (98%)
  between operations  0.64 us (2%)
    pallas_call x1, Pallas kernels, body(): pl.pallas_call(functools.partial(exchange, n), out_shape=(pltpu.VMEM(((OW...  31.4 us
    pallas_call x1, Pallas kernels, body(): pl.pallas_call(finish, out_shape=(jax.ShapeDtypeStruct((OWN, K), f32), ja...  3.27 us

profile of v3, /device:TPU:1, one launch (start us, length us, event | category | flops | bytes accessed | tf_op | source)
XLA Modules:
  0.0 35.3 jit_solution(15560651583687350210)
XLA Ops:
  0.6 31.4 %exchange.1 = (f32[224,8,128]{2,1,0:T(8,128)S(1)}, f32[7,32,2048]{2,1,0:T(8,128)S(1)}, s32[2,4,16]{2,1,0:T(4,128)S(1)}, s32[2,4,16]{2,1,0:T(4,128)S(1)}, s32[2,1,4]{2,1,0:T(1,128)S(1)}) custom-call(f32[4,32,2048]{2,1,0:T(8,128)} %inv_hbm.1, bf16[64,32,512]{2,1,0:T(8,128)(2,1)} %bitcast.2, f32[4,16,32]{2,1,0:T(8,128)} %old_ref.1, bf16[4,16,64]{2,1,0:T(8,128)(2,1)} %wts_ref.1, ...), custom_call_target="tpu_custom_call" | custom-call | tf_op jit(solution)/shard_map/exchange/pallas_call | solution.py:324
  32.0 3.3 %finish.1 = (f32[4,16]{1,0:T(4,128)}, f32[4,32,2048]{2,1,0:T(8,128)}) custom-call(f32[224,8,128]{2,1,0:T(8,128)S(1)} %get-tuple-element.7.rows_ref, f32[7,32,2048]{2,1,0:T(8,128)S(1)} %get-tuple-element.8.inv_ref, s32[2,4,16]{2,1,0:T(4,128)S(1)} %get-tuple-element.9.elec_ref, s32[2,4,16]{2,1,0:T(4,128)S(1)} %get-tuple-element.10.acc_ref, ...), custom_call_target="tpu_custom_call" | custom-call | tf_op jit(solution)/shard_map/finish/pallas_call | solution.py:362

commit v4 on v3

--- a/solution.py
+++ b/solution.py
@@ -13,8 +13,8 @@
 OTHER = 3
 K = 16
 BLOCKS = 16
-PAIRS = 2
-TILES = 64
+PAIRS = 1
+TILES = 128 // PAIRS
 WALK = 32
 
 
@@ -23,31 +23,43 @@
     return high, (x - high.astype(jnp.float32)).astype(jnp.bfloat16)
 
 
-def each_peer(me, n, sign, visit):
+def each_peer(me, n, sign, visit, far=False):
     if n != 64:
         for step in range(1, n):
             visit(step, lax.rem(me + sign * step + n, n))
         return
     z, y, x = lax.div(me, 16), lax.rem(lax.div(me, 4), 4), lax.rem(me, 4)
-    xs = [lax.rem(x + sign * move + 4, 4) for move in range(4)]
-    for move in range(1, 4):
-        visit(move, z * 16 + y * 4 + xs[move])
+    moves = (2, 3, 1, 0) if far else (0, 1, 3, 2)
+    xs = {move: lax.rem(x + sign * move + 4, 4) for move in moves}
+
+    def own():
+        for move in moves:
+            if move:
+                visit(move, z * 16 + y * 4 + xs[move])
 
     def line(index, carry):
-        high = lax.rem(z + sign * lax.div(index, 4) + 4, 4)
-        low = lax.rem(y + sign * lax.rem(index, 4) + 4, 4)
-        for move in range(4):
-            visit(index * 4 + move, high * 16 + low * 4 + xs[move])
+        index = 15 - index if far else index
+        high, low = lax.div(index, 4), lax.rem(index, 4)
+        high = high + lax.div(high, 2) * (5 - 2 * high)
+        low = low + lax.div(low, 2) * (5 - 2 * low)
+        base = 16 * lax.rem(z + sign * high + 4, 4) + 4 * lax.rem(y + sign * low + 4, 4)
+        for move in moves:
+            visit(high * 16 + low * 4 + move, base + xs[move])
         return carry
 
-    lax.fori_loop(1, 16, line, 0)
+    if far:
+        lax.fori_loop(0, 15, line, 0)
+        own()
+    else:
+        own()
+        lax.fori_loop(1, 16, line, 0)
 
 
 def exchange(
     n,
     inv_hbm, table_hbm, old_ref, wts_ref, tile_ref, elec_ref, acc_ref, off_ref,
-    rows_out, inv_out, elec_out, acc_out, off_out,
-    table, term, parts, tiles,
+    rows_out, inv_out, lanes, left_out,
+    elec_out, acc_out, off_out, table, term, parts, tiles,
     load_sem, inv_send, inv_recv, int_send, int_recv,
     rs_send, rs_recv, ag_send, ag_recv, fw_send, fw_recv,
 ):
@@ -59,9 +71,13 @@
 
     barrier = pltpu.get_barrier_semaphore()
 
-    load_inv = pltpu.make_async_copy(inv_hbm, inv_out.at[pl.ds(0, OWN)], load_sem.at[0])
-    load_table = pltpu.make_async_copy(table_hbm, table, load_sem.at[1])
-    load_table.start()
+    load_inv = pltpu.make_async_copy(inv_hbm, inv_out.at[pl.ds(0, OWN)], load_sem.at[4])
+    load_table = [
+        pltpu.make_async_copy(table_hbm.at[pl.ds(16 * c, 16)], table.at[pl.ds(16 * c, 16)], load_sem.at[c])
+        for c in range(4)
+    ]
+    for load in load_table:
+        load.start()
     load_inv.start()
 
     pl.semaphore_signal(barrier, inc=1, device_id=partner, device_id_type=MESH)
@@ -69,7 +85,7 @@
     def greet(step, peer):
         pl.semaphore_signal(barrier, inc=1, device_id={"orb": peer}, device_id_type=MESH)
 
-    each_peer(me, n, 1, greet)
+    each_peer(me, n, 1, greet, True)
 
     elec_out[0] = elec_ref[...]
     acc_out[0] = acc_ref[...]
@@ -80,10 +96,11 @@
     ids = tiles[0:1, 0:OWN * K]
     pick = (lax.broadcasted_iota(jnp.int32, (512, OWN * K), 0) == ids).astype(jnp.float32).astype(jnp.bfloat16)
     weights = wts_ref[...].reshape(OWN * K, 64).astype(jnp.float32).T
-    load_table.wait()
     local = table.shape[1]
     total = jnp.zeros((local, OWN * K), jnp.float32)
     for chunk in range(0, 64, 8):
+        if chunk % 16 == 0:
+            load_table[chunk // 16].wait()
         block = table[chunk:chunk + 8].reshape(8 * local, 512)
         picked = jnp.dot(block, pick, preferred_element_type=jnp.float32)
         picked = picked.reshape(8, local, OWN * K)
@@ -93,8 +110,8 @@
     load_inv.wait()
 
     def project(pair):
-        for index in range(2):
-            walker = 2 * pair + index
+        for index in range(OWN // PAIRS):
+            walker = OWN // PAIRS * pair + index
             high, low = halves(change[walker * K:(walker + 1) * K])
             left = jnp.concatenate([high, high, low], axis=1)
             for block in range(0, BLOCKS, 4):
@@ -115,7 +132,7 @@
                 device_id={"orb": peer}, device_id_type=MESH,
             ).start()
 
-        each_peer(me, n, 1, visit)
+        each_peer(me, n, 1, visit, True)
 
     project(0)
     pl.semaphore_wait(barrier, n)
@@ -138,14 +155,15 @@
     for copy in copies:
         copy.start()
 
-    project(1)
-    scatter(1)
+    for pair in range(1, PAIRS):
+        project(pair)
+        scatter(pair)
 
     def place(pair, owner):
         return pair * TILES + owner * share
 
     def forward(pair, owner):
-        walker = 2 * pair + lax.div(owner * share, WALK)
+        walker = OWN // PAIRS * pair + lax.div(owner * share, WALK)
         wanted = jnp.logical_and(walker >= first, walker < first + OTHER)
 
         @pl.when(wanted)
@@ -171,8 +189,33 @@
                 device_id={"orb": peer}, device_id_type=MESH,
             ).start()
 
-        each_peer(me, n, 1, gather)
+        each_peer(me, n, 1, gather, True)
         forward(pair, me)
+
+    for copy in copies:
+        copy.wait()
+
+    lanes[...] = jnp.zeros_like(lanes)
+    for slot in range(OWN + OTHER):
+        for row, ref in enumerate((elec_out, acc_out)):
+            if slot < OWN:
+                value = ref[0, slot:slot + 1, :]
+            else:
+                value = ref[1, pl.ds(slot - OWN + core, 1), :]
+            lanes[row:row + 1, slot * K:(slot + 1) * K] = value
+    for row in range(2):
+        lanes[2 + row:3 + row, 0:OWN] = off_out[row]
+
+    elec = lanes[0:1, :]
+    lane = lax.broadcasted_iota(jnp.int32, (1, 128), 1)
+    wide = jnp.broadcast_to(elec % 128, (local, 128))
+    columns = jnp.zeros((local, 128), jnp.float32)
+    for slot in range(OWN + OTHER):
+        for block in range(BLOCKS):
+            hit = jnp.logical_and(lane // K == slot, elec // 128 == block)
+            got = jnp.take_along_axis(inv_out[slot, :, block * 128:(block + 1) * 128], wide, axis=1)
+            columns = jnp.where(hit, got, columns)
+    left_out[...] = columns
 
     for pair in range(PAIRS):
         def arrive(step, owner):
@@ -182,8 +225,6 @@
 
         each_peer(me, n, -1, arrive)
 
-    for copy in copies:
-        copy.wait()
     for pair in range(PAIRS):
         pltpu.make_async_copy(rest[pair], rest[pair], rs_send.at[pair]).wait()
         pltpu.make_async_copy(rest[pair], rest[pair], ag_send.at[pair]).wait()
@@ -192,28 +233,19 @@
     pltpu.make_async_copy(moved, moved, fw_recv).wait()
 
 
-def finish(rows_ref, inv_ref, elec_ref, acc_ref, off_ref, ratio_ref, out_hbm, lanes, out_ref, out_sem):
+def finish(rows_ref, inv_ref, lanes, left_ref, ratio_ref, out_hbm, out_ref, out_sem):
     core = lax.axis_index("walk")
     local = inv_ref.shape[1]
     count = OWN + OTHER
 
-    lanes[...] = jnp.zeros_like(lanes)
-    for slot in range(count):
-        for row, ref in enumerate((elec_ref, acc_ref)):
-            if slot < OWN:
-                value = ref[0, slot:slot + 1, :]
-            else:
-                value = ref[1, pl.ds(slot - OWN + core, 1), :]
-            lanes[row:row + 1, slot * K:(slot + 1) * K] = value
     elec = lanes[0:1, :]
     lane = lax.broadcasted_iota(jnp.int32, (1, 128), 1)
     group, move = lane // K, lane % K
     spot = jnp.broadcast_to(elec % 128, (K, 128))
     home = elec // 128
 
+    left = left_ref[...]
     cross = jnp.zeros((K, 128), jnp.float32)
-    left = jnp.zeros((local, 128), jnp.float32)
-    wide = jnp.broadcast_to(elec % 128, (local, 128))
     for slot in range(count):
         for block in range(BLOCKS):
             hit = jnp.logical_and(group == slot, home == block)
@@ -221,8 +253,6 @@
                 rows_ref[pl.ds(slot * WALK + block * 2, 2)].reshape(K, 128), spot, axis=1
             )
             cross = jnp.where(hit, got, cross)
-            got = jnp.take_along_axis(inv_ref[slot, :, block * 128:(block + 1) * 128], wide, axis=1)
-            left = jnp.where(hit, got, left)
 
     rowid = lax.broadcasted_iota(jnp.int32, (K, 128), 0)
     full = cross + jnp.where(rowid == move, 1.0, 0.0)
@@ -260,8 +290,6 @@
     w8 = lax.broadcasted_iota(jnp.int32, (8, 128), 0)
     counts = jnp.zeros((8, 128), jnp.int32)
     lane8 = lax.broadcasted_iota(jnp.int32, (8, 128), 1)
-    lanes[2:3, 0:OWN] = off_ref[0]
-    lanes[3:4, 0:OWN] = off_ref[1]
     mine = lanes[2:3, :]
     theirs = lanes[3:4, :]
     low = jnp.where(core == 0, mine, theirs)
@@ -321,23 +349,25 @@
     vmem = pl.BlockSpec(memory_space=pltpu.VMEM)
     anywhere = pl.BlockSpec(memory_space=pl.ANY)
     f32, i32 = jnp.float32, jnp.int32
-    rows, inv_all, elec_all, acc_all, off_all = pl.pallas_call(
+    kept = pl.pallas_call(
         functools.partial(exchange, n),
         out_shape=(
             pltpu.VMEM(((OWN + OTHER) * WALK, 8, 128), f32),
             pltpu.VMEM((OWN + OTHER, local, 2048), f32),
+            pltpu.VMEM((8, 128), i32),
+            pltpu.VMEM((local, 128), f32),
+        ),
+        in_specs=[anywhere, anywhere] + [vmem] * 6,
+        out_specs=(vmem,) * 4,
+        scratch_shapes=[
             pltpu.VMEM((2, OWN, K), i32),
             pltpu.VMEM((2, OWN, K), i32),
             pltpu.VMEM((2, 1, OWN), i32),
-        ),
-        in_specs=[anywhere, anywhere] + [vmem] * 6,
-        out_specs=(vmem,) * 5,
-        scratch_shapes=[
             pltpu.VMEM((64, local, 512), jnp.bfloat16),
             pltpu.VMEM((PAIRS, TILES, 8, 128), f32),
             pltpu.VMEM((PAIRS, n, share, 8, 128), f32),
             pltpu.VMEM((8, 128), i32),
-            pltpu.SemaphoreType.DMA((2,)),
+            pltpu.SemaphoreType.DMA((5,)),
             pltpu.SemaphoreType.DMA,
             pltpu.SemaphoreType.DMA,
             pltpu.SemaphoreType.DMA((3,)),
@@ -357,7 +387,7 @@
     )
     kept = [
         pltpu.with_memory_space_constraint(x, pltpu.VMEM)
-        for x in (rows, inv_all, elec_all, acc_all, off_all)
+        for x in kept
     ]
     ratios, new_inverse = pl.pallas_call(
         finish,
@@ -365,10 +395,9 @@
             jax.ShapeDtypeStruct((OWN, K), f32),
             jax.ShapeDtypeStruct((OWN, local, 2048), f32),
         ),
-        in_specs=[vmem] * 5,
+        in_specs=[vmem] * 4,
         out_specs=(vmem, anywhere),
         scratch_shapes=[
-            pltpu.VMEM((8, 128), i32),
             pltpu.VMEM((OWN, local, 2048), f32),
             pltpu.SemaphoreType.DMA,
         ],

time: 35.4 us -> 34 us (0.960)
  Pallas kernels: 34.6 us -> 33.2 us
    pallas_call x1, Pallas kernels: 31.4 us -> 30.3 us  [body(): pl.pallas_call(functools.partial(exchange, n), out_shape=(pltpu.VMEM(((OW...]
    pallas_call x1, Pallas kernels: 3.27 us -> 2.88 us  [body(): pl.pallas_call(finish, out_shape=(jax.ShapeDtypeStruct((OWN, K), f32), ja...]
where the time goes in v4:
time: 34 us; the launch traced here: 33.8 us
  Pallas kernels  33.2 us (98%)
  between operations  0.64 us (2%)
    pallas_call x1, Pallas kernels, body(): pl.pallas_call(functools.partial(exchange, n), out_shape=(pltpu.VMEM(((OW...  30.3 us
    pallas_call x1, Pallas kernels, body(): pl.pallas_call(finish, out_shape=(jax.ShapeDtypeStruct((OWN, K), f32), ja...  2.88 us

profile of v4, /device:TPU:1, one launch (start us, length us, event | category | flops | bytes accessed | tf_op | source)
XLA Modules:
  0.0 33.8 jit_solution(14799133757944407063)
XLA Ops:
  0.6 30.3 %exchange.1 = (f32[224,8,128]{2,1,0:T(8,128)S(1)}, f32[7,32,2048]{2,1,0:T(8,128)S(1)}, s32[8,128]{1,0:T(8,128)S(1)}, f32[32,128]{1,0:T(8,128)S(1)}) custom-call(f32[4,32,2048]{2,1,0:T(8,128)} %inv_hbm.1, bf16[64,32,512]{2,1,0:T(8,128)(2,1)} %bitcast.2, f32[4,16,32]{2,1,0:T(8,128)} %old_ref.1, bf16[4,16,64]{2,1,0:T(8,128)(2,1)} %wts_ref.1, s32[4,16]{1,0:T(4,128)} %tile_ref.1, ...), custom_call_target="tpu_custom_call" | custom-call | tf_op jit(solution)/shard_map/exchange/pallas_call | solution.py:352
  31.0 2.9 %finish.1 = (f32[4,16]{1,0:T(4,128)}, f32[4,32,2048]{2,1,0:T(8,128)}) custom-call(f32[224,8,128]{2,1,0:T(8,128)S(1)} %get-tuple-element.6.rows_ref, f32[7,32,2048]{2,1,0:T(8,128)S(1)} %get-tuple-element.7.inv_ref, s32[8,128]{1,0:T(8,128)S(1)} %get-tuple-element.8.lanes, f32[32,128]{1,0:T(8,128)S(1)} %get-tuple-element.9.left_ref), custom_call_target="tpu_custom_call" | custom-call | tf_op jit(solution)/shard_map/finish/pallas_call | solution.py:392

commit v5 on v4

--- a/solution.py
+++ b/solution.py
@@ -23,36 +23,29 @@
     return high, (x - high.astype(jnp.float32)).astype(jnp.bfloat16)
 
 
-def each_peer(me, n, sign, visit, far=False):
+def hops(step):
+    return sum(min(d, 4 - d) for d in (step // 16, step // 4 % 4, step % 4))
+
+
+def diagonal(i, m):
+    return (i // 4 + m) % 4 * 16 + (i % 4 + m) % 4 * 4 + m
+
+
+MIXED = [diagonal(i, m) for i in range(16) for m in range(4) if i or m]
+FAR = sorted(MIXED, key=lambda step: -hops(step))
+
+
+def each_peer(me, n, sign, visit, order=FAR):
     if n != 64:
         for step in range(1, n):
             visit(step, lax.rem(me + sign * step + n, n))
         return
-    z, y, x = lax.div(me, 16), lax.rem(lax.div(me, 4), 4), lax.rem(me, 4)
-    moves = (2, 3, 1, 0) if far else (0, 1, 3, 2)
-    xs = {move: lax.rem(x + sign * move + 4, 4) for move in moves}
-
-    def own():
-        for move in moves:
-            if move:
-                visit(move, z * 16 + y * 4 + xs[move])
-
-    def line(index, carry):
-        index = 15 - index if far else index
-        high, low = lax.div(index, 4), lax.rem(index, 4)
-        high = high + lax.div(high, 2) * (5 - 2 * high)
-        low = low + lax.div(low, 2) * (5 - 2 * low)
-        base = 16 * lax.rem(z + sign * high + 4, 4) + 4 * lax.rem(y + sign * low + 4, 4)
-        for move in moves:
-            visit(high * 16 + low * 4 + move, base + xs[move])
-        return carry
-
-    if far:
-        lax.fori_loop(0, 15, line, 0)
-        own()
-    else:
-        own()
-        lax.fori_loop(1, 16, line, 0)
+    digits = [
+        [scale * lax.rem(lax.rem(lax.div(me, scale), 4) + sign * move + 4, 4) for move in range(4)]
+        for scale in (16, 4, 1)
+    ]
+    for step in order:
+        visit(step, digits[0][step // 16] + digits[1][step // 4 % 4] + digits[2][step % 4])
 
 
 def exchange(
@@ -85,7 +78,7 @@
     def greet(step, peer):
         pl.semaphore_signal(barrier, inc=1, device_id={"orb": peer}, device_id_type=MESH)
 
-    each_peer(me, n, 1, greet, True)
+    each_peer(me, n, 1, greet)
 
     elec_out[0] = elec_ref[...]
     acc_out[0] = acc_ref[...]
@@ -132,7 +125,7 @@
                 device_id={"orb": peer}, device_id_type=MESH,
             ).start()
 
-        each_peer(me, n, 1, visit, True)
+        each_peer(me, n, 1, visit)
 
     project(0)
     pl.semaphore_wait(barrier, n)
@@ -189,7 +182,7 @@
                 device_id={"orb": peer}, device_id_type=MESH,
             ).start()
 
-        each_peer(me, n, 1, gather, True)
+        each_peer(me, n, 1, gather)
         forward(pair, me)
 
     for copy in copies:

time: 34 us -> 33.4 us (0.982)
  Pallas kernels: 33.2 us -> 32.6 us
    pallas_call x1, Pallas kernels: 30.3 us -> 29.7 us  [body(): pl.pallas_call(functools.partial(exchange, n), out_shape=(pltpu.VMEM(((OW...]
where the time goes in v5:
time: 33.4 us; the launch traced here: 33.2 us
  Pallas kernels  32.6 us (98%)
  between operations  0.64 us (2%)
    pallas_call x1, Pallas kernels, body(): pl.pallas_call(functools.partial(exchange, n), out_shape=(pltpu.VMEM(((OW...  29.7 us
    pallas_call x1, Pallas kernels, body(): pl.pallas_call(finish, out_shape=(jax.ShapeDtypeStruct((OWN, K), f32), ja...  2.89 us

profile of v5, /device:TPU:1, one launch (start us, length us, event | category | flops | bytes accessed | tf_op | source)
XLA Modules:
  0.0 33.2 jit_solution(421955653770870435)
XLA Ops:
  0.6 29.7 %exchange.1 = (f32[224,8,128]{2,1,0:T(8,128)S(1)}, f32[7,32,2048]{2,1,0:T(8,128)S(1)}, s32[8,128]{1,0:T(8,128)S(1)}, f32[32,128]{1,0:T(8,128)S(1)}) custom-call(f32[4,32,2048]{2,1,0:T(8,128)} %inv_hbm.1, bf16[64,32,512]{2,1,0:T(8,128)(2,1)} %bitcast.2, f32[4,16,32]{2,1,0:T(8,128)} %old_ref.1, bf16[4,16,64]{2,1,0:T(8,128)(2,1)} %wts_ref.1, s32[4,16]{1,0:T(4,128)} %tile_ref.1, ...), custom_call_target="tpu_custom_call" | custom-call | tf_op jit(solution)/shard_map/exchange/pallas_call | solution.py:345
  30.4 2.9 %finish.1 = (f32[4,16]{1,0:T(4,128)}, f32[4,32,2048]{2,1,0:T(8,128)}) custom-call(f32[224,8,128]{2,1,0:T(8,128)S(1)} %get-tuple-element.6.rows_ref, f32[7,32,2048]{2,1,0:T(8,128)S(1)} %get-tuple-element.7.inv_ref, s32[8,128]{1,0:T(8,128)S(1)} %get-tuple-element.8.lanes, f32[32,128]{1,0:T(8,128)S(1)} %get-tuple-element.9.left_ref), custom_call_target="tpu_custom_call" | custom-call | tf_op jit(solution)/shard_map/finish/pallas_call | solution.py:385
